TPU v7x, 512 devices: a whole 4x8x8 slice. The times are simulated.
512 devices in a mesh: dp: 16 (over z, core), mp: 32 (over y, x).
Axes of the slice: x: 4, y: 8, z: 8, core: 2. Of those that a mesh axis runs over, the one named last changes fastest.
Arguments:
- policy_hidden: bfloat16 [1024, 3584], P('dp'), may hold values from -96 to 96
- reference_hidden: bfloat16 [1024, 3584], P('dp'), may hold values from -96 to 96
- policy_gain: float32 [3584], replicated, may hold values from 0.5 to 1.5
- reference_gain: float32 [3584], replicated, may hold values from 0.5 to 1.5
- policy_embedding: bfloat16 [131072, 3584], P(('dp', 'mp')), may hold values from -1 to 1
- reference_embedding: bfloat16 [131072, 3584], P(('dp', 'mp')), may hold values from -1 to 1
- mixture_weight: float32 [1024], replicated, may hold values from 0.1 to 0.9
- sampled_tokens: int32 [1024], replicated, may hold values from 0 to 131071
Outputs:
- mixture_shift: float32 [1024, 131072], P(None, ('dp', 'mp'))
- sampled_logprobs: float32 [3, 1024], P(None, 'dp')
All inputs are finite; a program needn't handle non-finite values.
Results may differ from a plain program's by a relative error of at most 0.002.
Values may be sent and summed in bfloat16 or wider, within the bound.
No kernel may reach another device: no remote copies, remote signals or barrier semaphores. Data moves between devices by JAX's collectives and lax.ppermute only.
A program may use at most 64 MiB of HBM per device.

v0:
```python
import jax
import jax.numpy as jnp
from jax import lax
from jax.sharding import Mesh
from jax.sharding import PartitionSpec as P

DP = ("dp_0", "dp_1")
MP = ("mp_0", "mp_1")
DP_MP = ("dp_0", "dp_1", "mp_0", "mp_1")
softcap = 30.0
epsilon = 1e-06


def by_axis(x, axes):
    for axis in axes:
        x = lax.psum(x, axis)
    return x


def normalize(hidden, gain):
    values = hidden.astype(jnp.float32)
    meansq = jnp.mean(values * values, axis=-1, keepdims=True)
    return (values * lax.rsqrt(meansq + epsilon) * gain).astype(jnp.bfloat16)


def contract(normed, embedding):
    return lax.dot_general(
        normed, embedding, (((1,), (1,)), ((), ())), preferred_element_type=jnp.float32
    )


def local(
    policy_hidden,
    reference_hidden,
    policy_gain,
    reference_gain,
    policy_embedding,
    reference_embedding,
    mixture_weight,
    sampled_tokens,
):
    seq_local = policy_hidden.shape[0]
    vocab_local = policy_embedding.shape[0]
    stacked = jnp.stack(
        [normalize(policy_hidden, policy_gain), normalize(reference_hidden, reference_gain)]
    )
    piece = lax.all_gather(stacked, DP, axis=1, tiled=True)
    raw = jnp.stack([contract(piece[0], policy_embedding), contract(piece[1], reference_embedding)])
    capped = softcap * jnp.tanh(raw / softcap)
    capped_policy = capped[0]
    capped_reference = capped[1]
    weight = mixture_weight[:, None]
    mixed = (1.0 - weight) * capped_policy + weight * capped_reference
    shard = lax.axis_index(DP) * lax.axis_size(MP) + lax.axis_index(MP)
    first = shard * vocab_local
    columns = lax.broadcasted_iota(jnp.int32, (1, vocab_local), 1)
    onehot = (sampled_tokens[:, None] - first == columns).astype(jnp.float32)
    terms = (
        jnp.sum(jnp.exp(capped_policy), axis=1),
        jnp.sum(jnp.exp(capped_reference), axis=1),
        jnp.sum(jnp.exp(mixed), axis=1),
        jnp.sum(onehot * capped_policy, axis=1),
        jnp.sum(onehot * capped_reference, axis=1),
    )
    policy_sum, reference_sum, mixture_sum, policy_pick, reference_pick = (
        by_axis(terms[0], DP_MP),
        by_axis(terms[1], DP_MP),
        by_axis(terms[2], DP_MP),
        by_axis(terms[3], DP_MP),
        by_axis(terms[4], DP_MP),
    )
    policy_total = jnp.log(policy_sum)
    reference_total = jnp.log(reference_sum)
    mixture_total = jnp.log(mixture_sum)
    mixed_pick = (1.0 - mixture_weight) * policy_pick + mixture_weight * reference_pick
    policy_logp = policy_pick - policy_total
    reference_logp = reference_pick - reference_total
    mixture_logp = mixed_pick - mixture_total
    mixture_shift = mixed - mixture_total[:, None] - (capped_policy - policy_total[:, None])
    every_logp = jnp.stack([policy_logp, reference_logp, mixture_logp])
    sampled_logprobs = lax.dynamic_slice_in_dim(
        every_logp, lax.axis_index(DP) * seq_local, seq_local, 1
    )
    return (mixture_shift, sampled_logprobs)


def solution(mesh):
    split = Mesh(mesh.devices.reshape(8, 2, 8, 4), ("dp_0", "dp_1", "mp_0", "mp_1"))
    in_specs = (P(DP, None), P(DP, None), P(), P(), P(DP_MP, None), P(DP_MP, None), P(), P())
    out_specs = (P(None, DP_MP), P(None, DP))
    return jax.shard_map(local, mesh=split, in_specs=in_specs, out_specs=out_specs, check_vma=False)
```

profile of v0, /device:TPU:4, one launch (start us, length us, event | category | flops | bytes accessed | tf_op | source)
XLA Modules:
  0.0 205.5 jit_solution(13288046181011595460)
XLA Ops:
  7.2 0.0 copy-start
  7.2 0.0 all-gather.2.cloned.1.call-start
  7.2 1.3 fusion.9
  8.6 1.2 fusion.6
  9.8 0.0 copy-start.2
  9.8 0.0 copy-start.3
  9.8 1.5 fusion.12
  11.3 1.0 pad_maximum_fusion
  12.3 0.0 all-gather.2.cloned.1.call-update
  12.4 93.7 %all-gather.2.cloned.1.call-done = bf16[2,1024,3584]{2,1,0:T(8,128)(2,1)} async-done(((bf16[2,64,3584]{2,1,0:T(8,128)(2,1)}), bf16[2,1024,3584]{2,1,0:T(8,128)(2,1)}) %all-gather.2.cloned.1.call-update) | async-done | bytes 14680080 | tf_op jit(solution)/shard_map/all_gather | solution.py:47
  106.1 5.3 %fusion.5 = f32[1,1024,256]{1,2,0:T(8,128)S(1)} fusion(bf16[256,3584]{1,0:T(8,128)(2,1)S(1)} %copy-done, bf16[2,1024,3584]{2,1,0:T(8,128)(2,1)} %all-gather.2.cloned.1.call-done), kind=kOutput, calls=%fused_computation.8 | convolution fusion | flops 1879048192 | bytes 10223616 | tf_op jit(solution)/shard_map/dot_general | solution.py:27
  111.4 1.9 copy-done.4
  113.3 0.5 copy-done.5
  113.9 2.1 %fusion.4 = f32[1,1024,256]{1,2,0:T(8,128)S(1)} fusion(bf16[256,3584]{1,0:T(8,128)(2,1)S(1)} %copy-done.5, bf16[2,1024,3584]{2,1,0:T(8,128)(2,1)S(1)} %copy-done.4), kind=kOutput, calls=%fused_computation.7 | convolution fusion | flops 1879048192 | bytes 10223616 | tf_op jit(solution)/shard_map/dot_general | solution.py:27
  115.9 0.3 fusion.3
  116.2 1.3 copy-done.1
  117.6 0.6 select_reduce_fusion
  118.2 28.2 %all-reduce.1 = (f32[1024]{0:T(1024)S(1)}, f32[1024]{0:T(1024)S(1)}, f32[1024]{0:T(1024)S(1)}, f32[1024]{0:T(1024)S(1)}, f32[1024]{0:T(1024)S(1)}) all-reduce(f32[1024]{0:T(1024)S(1)} %get-tuple-element.8, f32[1024]{0:T(1024)S(1)} %get-tuple-element.7, ...), channel_id=1, replica_groups=mesh['dp_0'=8,'dp_1'=2,'mp_0'=8,'mp_1'=4] {'dp_0'}, use_global_device_ids=true, to_apply=%region_8.0 | all-reduce | flops 5120 | bytes 40960 | tf_op jit(solution)/shard_map/psum | solution.py:16
  146.4 3.4 %all-reduce.3 = (f32[1024]{0:T(1024)S(1)}, f32[1024]{0:T(1024)S(1)}, f32[1024]{0:T(1024)S(1)}, f32[1024]{0:T(1024)S(1)}, f32[1024]{0:T(1024)S(1)}) all-reduce(f32[1024]{0:T(1024)S(1)} %get-tuple-element.14, f32[1024]{0:T(1024)S(1)} %get-tuple-element.15, ...), channel_id=1, replica_groups=mesh['dp_0'=8,'dp_1'=2,'mp_0'=8,'mp_1'=4] {'dp_1'}, use_global_device_ids=true, to_apply=%region_9.0 | all-reduce | flops 5120 | bytes 40960 | tf_op jit(solution)/shard_map/psum | solution.py:16
  149.8 29.7 %all-reduce = (f32[1024]{0:T(1024)S(1)}, f32[1024]{0:T(1024)S(1)}, f32[1024]{0:T(1024)S(1)}, f32[1024]{0:T(1024)S(1)}, f32[1024]{0:T(1024)S(1)}) all-reduce(f32[1024]{0:T(1024)S(1)} %get-tuple-element.24, f32[1024]{0:T(1024)S(1)} %get-tuple-element.25, ...), channel_id=1, replica_groups=mesh['dp_0'=8,'dp_1'=2,'mp_0'=8,'mp_1'=4] {'mp_0'}, use_global_device_ids=true, to_apply=%region_10.0 | all-reduce | flops 5120 | bytes 40960 | tf_op jit(solution)/shard_map/psum | solution.py:16
  179.5 15.4 %all-reduce.2 = (f32[1024]{0:T(1024)S(1)}, f32[1024]{0:T(1024)S(1)}, f32[1024]{0:T(1024)S(1)}, f32[1024]{0:T(1024)S(1)}, f32[1024]{0:T(1024)S(1)}) all-reduce(f32[1024]{0:T(1024)S(1)} %get-tuple-element.9, f32[1024]{0:T(1024)S(1)} %get-tuple-element.10, ...), channel_id=1, replica_groups=mesh['dp_0'=8,'dp_1'=2,'mp_0'=8,'mp_1'=4] {'mp_1'}, use_global_device_ids=true, to_apply=%region_11.0 | all-reduce | flops 5120 | bytes 40960 | tf_op jit(solution)/shard_map/psum | solution.py:16
  194.9 1.8 subtract_subtract_fusion
  196.7 1.3 copy.10
  198.0 0.7 fusion.15
  (11 shorter events, 0.0 us)
Async XLA Ops:
  7.2 98.9 %copy-start = (bf16[256,3584]{1,0:T(8,128)(2,1)S(1)}, bf16[256,3584]{1,0:T(8,128)(2,1)}, u32[]{:S(2)}) copy-start(bf16[256,3584]{1,0:T(8,128)(2,1)} %param.13) | copy-start | bytes 5505028
  7.2 98.9 %all-gather.2.cloned.1.call-start = ((), (), s32[]{:S(2)}) async-start(), calls=%async_computation | async-start | bytes 15597568 | tf_op jit(solution)/shard_map/all_gather | solution.py:47
  9.8 2.6 %copy-start.2 = (f32[1024]{0:T(1024)S(1)}, f32[1024]{0:T(1024)}, u32[]{:S(2)}) copy-start(f32[1024]{0:T(1024)} %param.14) | copy-start | bytes 12292
  9.8 2.6 %copy-start.3 = (s32[1024]{0:T(1024)S(1)}, s32[1024]{0:T(1024)}, u32[]{:S(2)}) copy-start(s32[1024]{0:T(1024)} %param.15) | copy-start | bytes 12292
  106.1 7.3 %copy-start.4 = (bf16[2,1024,3584]{2,1,0:T(8,128)(2,1)S(1)}, bf16[2,1024,3584]{2,1,0:T(8,128)(2,1)}, u32[]{:S(2)}) copy-start(bf16[2,1024,3584]{2,1,0:T(8,128)(2,1)} %all-gather.2.cloned.1.call-done) | copy-start | bytes 44040196
  106.1 7.8 %copy-start.5 = (bf16[256,3584]{1,0:T(8,128)(2,1)S(1)}, bf16[256,3584]{1,0:T(8,128)(2,1)}, u32[]{:S(2)}) copy-start(bf16[256,3584]{1,0:T(8,128)(2,1)} %param.12) | copy-start | bytes 5505028
  116.2 1.4 copy-start.1
Sparse Core Ops, SparseCore 0:
  12.5 93.5 all-gather.1
where the time goes:
time: 206 us
  waiting for transfers between devices  93.7 us (45%)
  blocking collectives  76.7 us (37%)
  between operations  14.2 us (7%)
  other arithmetic  8.41 us (4%)
  matrix products  7.39 us (4%)
  local copies, waits for them, and re-layouts  5.12 us (2%)
    all_gather x1, waiting for transfers between devices, local(): piece = lax.all_gather(stacked, DP, axis=1, tiled=True)  93.7 us
    psum x4, blocking collectives, by_axis(): x = lax.psum(x, axis)  76.7 us
    dot_general x2, matrix products, contract(): lax.dot_general(normed, embedding, (((1,), (1,)), ((), ())), preferred_el...  7.39 us
    unnamed x13, local copies, waits for them, and re-layouts  5.12 us
  transfers between devices with their start and end apart: 1, of which 1 were waited for; matrix products, arithmetic and copies ran while one was open for 0% of the time, Pallas kernels for 0%

commit v1 on v0

--- a/solution.py
+++ b/solution.py
@@ -13,7 +13,7 @@
 
 def by_axis(x, axes):
     for axis in axes:
-        x = lax.psum(x, axis)
+        x = jnp.sum(lax.all_gather(x, axis), axis=0)
     return x
 
 

time: 206 us -> 444 us (2.16)
  the two profiles are of different devices: /device:TPU:4 before, /device:TPU:16 now
where the time goes in v1:
time: 444 us
  blocking collectives  315 us (71%)
  waiting for transfers between devices  93.6 us (21%)
  between operations  14.3 us (3%)
  other arithmetic  8.74 us (2%)
  matrix products  7.39 us (2%)
  local copies, waits for them, and re-layouts  5.36 us (1%)
    all_gather x20, blocking collectives, by_axis(): x = jnp.sum(lax.all_gather(x, axis), axis=0)  315 us
    all_gather x1, waiting for transfers between devices, local(): piece = lax.all_gather(stacked, DP, axis=1, tiled=True)  93.5 us
  transfers between devices with their start and end apart: 1, of which 1 were waited for; matrix products, arithmetic and copies ran while one was open for 0% of the time, Pallas kernels for 0%

profile of v1, /device:TPU:16, one launch (start us, length us, event | category | flops | bytes accessed | tf_op | source)
XLA Modules:
  0.0 443.9 jit_solution(18201611409883514248)
XLA Ops:
  12.4 93.5 %all-gather.22.cloned.1.call-done = bf16[2,1024,3584]{2,1,0:T(8,128)(2,1)} async-done(((bf16[2,64,3584]{2,1,0:T(8,128)(2,1)}), bf16[2,1024,3584]{2,1,0:T(8,128)(2,1)}) %all-gather.22.cloned.1.call-update) | async-done | bytes 14680080 | tf_op jit(solution)/shard_map/all_gather | solution.py:47
  106.0 5.3 %fusion.5 = f32[1,1024,256]{1,2,0:T(8,128)S(1)} fusion(bf16[256,3584]{1,0:T(8,128)(2,1)S(1)} %copy-done, bf16[2,1024,3584]{2,1,0:T(8,128)(2,1)} %all-gather.22.cloned.1.call-done), kind=kOutput, calls=%fused_computation.8 | convolution fusion | flops 1879048192 | bytes 10223616 | tf_op jit(solution)/shard_map/dot_general | solution.py:27
  111.3 1.9 copy-done.4
  113.7 2.1 fusion.4
  118.1 24.5 %all-gather.12 = f32[8192]{0:T(1024)S(1)} all-gather(f32[1024]{0:T(1024)S(1)} %get-tuple-element.8), channel_id=14, replica_groups=mesh['dp_0'=8,'dp_1'=2,'mp_0'=8,'mp_1'=4] {'dp_0'}, dimensions={0}, use_global_device_ids=true | all-gather | bytes 36864 | tf_op jit(solution)/shard_map/all_gather | solution.py:16
  142.6 1.8 all-gather.13
  144.4 25.4 %all-gather.14 = f32[8192]{0:T(1024)S(1)} all-gather(f32[1024]{0:T(1024)S(1)} %reduce_sum.262), channel_id=16, replica_groups=mesh['dp_0'=8,'dp_1'=2,'mp_0'=8,'mp_1'=4] {'mp_0'}, dimensions={0}, use_global_device_ids=true | all-gather | bytes 36864 | tf_op jit(solution)/shard_map/all_gather | solution.py:16
  169.8 12.2 %all-gather.15 = f32[4096]{0:T(1024)S(1)} all-gather(f32[1024]{0:T(1024)S(1)} %reduce_sum.263), channel_id=17, replica_groups=mesh['dp_0'=8,'dp_1'=2,'mp_0'=8,'mp_1'=4] {'mp_1'}, dimensions={0}, use_global_device_ids=true | all-gather | bytes 20480 | tf_op jit(solution)/shard_map/all_gather | solution.py:16
  182.1 24.5 %all-gather.8 = f32[8192]{0:T(1024)S(1)} all-gather(f32[1024]{0:T(1024)S(1)} %get-tuple-element.9), channel_id=10, replica_groups=mesh['dp_0'=8,'dp_1'=2,'mp_0'=8,'mp_1'=4] {'dp_0'}, dimensions={0}, use_global_device_ids=true | all-gather | bytes 36864 | tf_op jit(solution)/shard_map/all_gather | solution.py:16
  206.6 1.8 all-gather.9
  208.4 24.5 %all-gather.10 = f32[8192]{0:T(1024)S(1)} all-gather(f32[1024]{0:T(1024)S(1)} %reduce_sum.257), channel_id=12, replica_groups=mesh['dp_0'=8,'dp_1'=2,'mp_0'=8,'mp_1'=4] {'mp_0'}, dimensions={0}, use_global_device_ids=true | all-gather | bytes 36864 | tf_op jit(solution)/shard_map/all_gather | solution.py:16
  232.9 11.9 %all-gather.11 = f32[4096]{0:T(1024)S(1)} all-gather(f32[1024]{0:T(1024)S(1)} %reduce_sum.258), channel_id=13, replica_groups=mesh['dp_0'=8,'dp_1'=2,'mp_0'=8,'mp_1'=4] {'mp_1'}, dimensions={0}, use_global_device_ids=true | all-gather | bytes 20480 | tf_op jit(solution)/shard_map/all_gather | solution.py:16
  244.9 24.5 %all-gather = f32[8192]{0:T(1024)S(1)} all-gather(f32[1024]{0:T(1024)S(1)} %get-tuple-element.11), channel_id=2, replica_groups=mesh['dp_0'=8,'dp_1'=2,'mp_0'=8,'mp_1'=4] {'dp_0'}, dimensions={0}, use_global_device_ids=true | all-gather | bytes 36864 | tf_op jit(solution)/shard_map/all_gather | solution.py:16
  269.4 1.8 all-gather.1
  271.2 24.5 %all-gather.2 = f32[8192]{0:T(1024)S(1)} all-gather(f32[1024]{0:T(1024)S(1)} %reduce_sum.247), channel_id=4, replica_groups=mesh['dp_0'=8,'dp_1'=2,'mp_0'=8,'mp_1'=4] {'mp_0'}, dimensions={0}, use_global_device_ids=true | all-gather | bytes 36864 | tf_op jit(solution)/shard_map/all_gather | solution.py:16
  295.7 11.9 %all-gather.3 = f32[4096]{0:T(1024)S(1)} all-gather(f32[1024]{0:T(1024)S(1)} %reduce_sum.248), channel_id=5, replica_groups=mesh['dp_0'=8,'dp_1'=2,'mp_0'=8,'mp_1'=4] {'mp_1'}, dimensions={0}, use_global_device_ids=true | all-gather | bytes 20480 | tf_op jit(solution)/shard_map/all_gather | solution.py:16
  307.7 24.5 %all-gather.4 = f32[8192]{0:T(1024)S(1)} all-gather(f32[1024]{0:T(1024)S(1)} %get-tuple-element.12), channel_id=6, replica_groups=mesh['dp_0'=8,'dp_1'=2,'mp_0'=8,'mp_1'=4] {'dp_0'}, dimensions={0}, use_global_device_ids=true | all-gather | bytes 36864 | tf_op jit(solution)/shard_map/all_gather | solution.py:16
  332.2 1.8 all-gather.5
  334.0 24.5 %all-gather.6 = f32[8192]{0:T(1024)S(1)} all-gather(f32[1024]{0:T(1024)S(1)} %reduce_sum.252), channel_id=8, replica_groups=mesh['dp_0'=8,'dp_1'=2,'mp_0'=8,'mp_1'=4] {'mp_0'}, dimensions={0}, use_global_device_ids=true | all-gather | bytes 36864 | tf_op jit(solution)/shard_map/all_gather | solution.py:16
  358.5 11.9 %all-gather.7 = f32[4096]{0:T(1024)S(1)} all-gather(f32[1024]{0:T(1024)S(1)} %reduce_sum.253), channel_id=9, replica_groups=mesh['dp_0'=8,'dp_1'=2,'mp_0'=8,'mp_1'=4] {'mp_1'}, dimensions={0}, use_global_device_ids=true | all-gather | bytes 20480 | tf_op jit(solution)/shard_map/all_gather | solution.py:16
  370.5 24.5 %all-gather.16 = f32[8192]{0:T(1024)S(1)} all-gather(f32[1024]{0:T(1024)S(1)} %get-tuple-element.10), channel_id=18, replica_groups=mesh['dp_0'=8,'dp_1'=2,'mp_0'=8,'mp_1'=4] {'dp_0'}, dimensions={0}, use_global_device_ids=true | all-gather | bytes 36864 | tf_op jit(solution)/shard_map/all_gather | solution.py:16
  395.0 1.8 all-gather.17
  396.8 24.5 %all-gather.18 = f32[8192]{0:T(1024)S(1)} all-gather(f32[1024]{0:T(1024)S(1)} %reduce_sum.267), channel_id=20, replica_groups=mesh['dp_0'=8,'dp_1'=2,'mp_0'=8,'mp_1'=4] {'mp_0'}, dimensions={0}, use_global_device_ids=true | all-gather | bytes 36864 | tf_op jit(solution)/shard_map/all_gather | solution.py:16
  421.3 11.9 %all-gather.19 = f32[4096]{0:T(1024)S(1)} all-gather(f32[1024]{0:T(1024)S(1)} %reduce_sum.268), channel_id=21, replica_groups=mesh['dp_0'=8,'dp_1'=2,'mp_0'=8,'mp_1'=4] {'mp_1'}, dimensions={0}, use_global_device_ids=true | all-gather | bytes 20480 | tf_op jit(solution)/shard_map/all_gather | solution.py:16
  (67 shorter events, 12.2 us)
Async XLA Ops:
  7.2 98.8 %copy-start = (bf16[256,3584]{1,0:T(8,128)(2,1)S(1)}, bf16[256,3584]{1,0:T(8,128)(2,1)}, u32[]{:S(2)}) copy-start(bf16[256,3584]{1,0:T(8,128)(2,1)} %param.13) | copy-start | bytes 5505028
  7.2 98.8 %all-gather.22.cloned.1.call-start = ((), (), s32[]{:S(2)}) async-start(), calls=%async_computation | async-start | bytes 15597568 | tf_op jit(solution)/shard_map/all_gather | solution.py:47
  9.8 2.6 copy-start.2
  9.8 2.6 copy-start.3
  105.9 7.3 %copy-start.4 = (bf16[2,1024,3584]{2,1,0:T(8,128)(2,1)S(1)}, bf16[2,1024,3584]{2,1,0:T(8,128)(2,1)}, u32[]{:S(2)}) copy-start(bf16[2,1024,3584]{2,1,0:T(8,128)(2,1)} %all-gather.22.cloned.1.call-done) | copy-start | bytes 44040196
  106.0 7.8 %copy-start.5 = (bf16[256,3584]{1,0:T(8,128)(2,1)S(1)}, bf16[256,3584]{1,0:T(8,128)(2,1)}, u32[]{:S(2)}) copy-start(bf16[256,3584]{1,0:T(8,128)(2,1)} %param.12) | copy-start | bytes 5505028
  116.1 1.4 copy-start.1
Sparse Core Ops, SparseCore 0:
  12.5 93.4 all-gather.21

commit v2 on v0

--- a/solution.py
+++ b/solution.py
@@ -44,7 +44,9 @@
     stacked = jnp.stack(
         [normalize(policy_hidden, policy_gain), normalize(reference_hidden, reference_gain)]
     )
-    piece = lax.all_gather(stacked, DP, axis=1, tiled=True)
+    piece = jnp.concatenate(
+        lax.all_to_all(jnp.stack([stacked] * lax.axis_size(DP)), DP, 0, 0), axis=1
+    )
     raw = jnp.stack([contract(piece[0], policy_embedding), contract(piece[1], reference_embedding)])
     capped = softcap * jnp.tanh(raw / softcap)
     capped_policy = capped[0]

time: 206 us -> 436 us (2.12)
  waiting for transfers between devices: 93.7 us -> 319 us
  between operations: 14.2 us -> 0.8 us
  local copies, waits for them, and re-layouts: 5.12 us -> 15.7 us
  starting transfers between devices: 0.04 us -> 10.6 us
    all_to_all x0 -> x1, waiting for transfers between devices: none -> 319 us  [local(): lax.all_to_all(jnp.stack([stacked] * lax.axis_size(DP)), DP, 0, 0)]
    all_gather x1 -> x0, waiting for transfers between devices: 93.7 us -> none  [local(): piece = lax.all_gather(stacked, DP, axis=1, tiled=True)]
    all_to_all x0 -> x1, starting transfers between devices: none -> 10.6 us  [local(): lax.all_to_all(jnp.stack([stacked] * lax.axis_size(DP)), DP, 0, 0)]
    another operation x0 -> x1, local copies, waits for them, and re-layouts: none -> 6.89 us  [local(): jnp.stack([stacked] * lax.axis_size(DP))]
    slice x0 -> x1, local copies, waits for them, and re-layouts: none -> 6.18 us  [local(): piece[0]]
where the time goes in v2:
time: 436 us
  waiting for transfers between devices  319 us (73%)
  blocking collectives  77.9 us (18%)
  local copies, waits for them, and re-layouts  15.7 us (4%)
  starting transfers between devices  10.6 us (2%)
  other arithmetic  7.49 us (2%)
    all_to_all x1, waiting for transfers between devices, local(): lax.all_to_all(jnp.stack([stacked] * lax.axis_size(DP)), DP, 0, 0)  319 us
    psum x4, blocking collectives, by_axis(): x = lax.psum(x, axis)  77.9 us
    all_to_all x1, starting transfers between devices, local(): lax.all_to_all(jnp.stack([stacked] * lax.axis_size(DP)), DP, 0, 0)  10.6 us
  transfers between devices with their start and end apart: 1, of which 1 were waited for; matrix products, arithmetic and copies ran while one was open for 0% of the time, Pallas kernels for 0%

profile of v2, /device:TPU:4, one launch (start us, length us, event | category | flops | bytes accessed | tf_op | source)
XLA Modules:
  0.0 435.6 jit_solution(17446743777192592667)
XLA Ops:
  0.6 0.0 copy-start
  0.6 1.3 fusion.5
  2.0 1.2 fusion.2
  3.2 1.5 fusion.8
  4.7 0.1 pad_maximum_fusion
  4.8 6.9 %stack.25 = bf16[16,2,64,3584]{3,2,1,0:T(8,128)(2,1)} broadcast(bf16[2,64,3584]{2,1,0:T(8,128)(2,1)S(1)} %pad_maximum_fusion), dimensions={1,2,3} | broadcast | bytes 15597568 | tf_op jit(solution)/shard_map/stack | solution.py:48
  11.7 10.6 %all-to-all-start = ((bf16[16,2,64,3584]{3,2,1,0:T(8,128)(2,1)}), bf16[16,2,64,3584]{3,2,1,0:T(8,128)(2,1)}, u32[]{:S(2)}, u32[]{:S(2)}) async-start(bf16[16,2,64,3584]{3,2,1,0:T(8,128)(2,1)} %stack.25), calls=%async_computation | async-start | bytes 29360128 | tf_op jit(solution)/shard_map/all_to_all | solution.py:48
  22.3 0.0 copy-done.2
  22.3 0.0 copy-done.3
  22.4 318.9 %all-to-all-done = bf16[16,2,64,3584]{3,2,1,0:T(8,128)(2,1)} async-done(((bf16[16,2,64,3584]{3,2,1,0:T(8,128)(2,1)}), bf16[16,2,64,3584]{3,2,1,0:T(8,128)(2,1)}, u32[]{:S(2)}, u32[]{:S(2)}) %all-to-all-start) | async-done | bytes 14680096 | tf_op jit(solution)/shard_map/all_to_all | solution.py:48
  341.3 6.2 %fusion.12 = (bf16[1,16,64,3584]{3,2,0,1:T(8,128)(2,1)S(1)}, bf16[1,16,64,3584]{3,2,0,1:T(8,128)(2,1)S(1)}) fusion(bf16[2,16,64,3584]{3,2,0,1:T(8,128)(2,1)} %bitcast.2), kind=kLoop, calls=%fused_computation.40 | loop fusion | bytes 29360128 | tf_op jit(solution)/shard_map/slice | solution.py:50
  347.5 0.0 copy-start.4
  347.5 2.1 convolution_bitcast_fusion
  349.6 2.1 convolution_bitcast_fusion.1
  351.7 0.3 fusion.1
  352.0 1.3 copy-done.1
  353.3 0.6 select_reduce_fusion
  354.0 28.7 %all-reduce.1 = (f32[1024]{0:T(1024)S(1)}, f32[1024]{0:T(1024)S(1)}, f32[1024]{0:T(1024)S(1)}, f32[1024]{0:T(1024)S(1)}, f32[1024]{0:T(1024)S(1)}) all-reduce(f32[1024]{0:T(1024)S(1)} %get-tuple-element.8, f32[1024]{0:T(1024)S(1)} %get-tuple-element.7, ...), channel_id=1, replica_groups=mesh['dp_0'=8,'dp_1'=2,'mp_0'=8,'mp_1'=4] {'dp_0'}, use_global_device_ids=true, to_apply=%region_8.0 | all-reduce | flops 5120 | bytes 40960 | tf_op jit(solution)/shard_map/psum | solution.py:16
  382.7 3.4 all-reduce.3
  386.1 30.4 %all-reduce = (f32[1024]{0:T(1024)S(1)}, f32[1024]{0:T(1024)S(1)}, f32[1024]{0:T(1024)S(1)}, f32[1024]{0:T(1024)S(1)}, f32[1024]{0:T(1024)S(1)}) all-reduce(f32[1024]{0:T(1024)S(1)} %get-tuple-element.24, f32[1024]{0:T(1024)S(1)} %get-tuple-element.25, ...), channel_id=1, replica_groups=mesh['dp_0'=8,'dp_1'=2,'mp_0'=8,'mp_1'=4] {'mp_0'}, use_global_device_ids=true, to_apply=%region_10.0 | all-reduce | flops 5120 | bytes 40960 | tf_op jit(solution)/shard_map/psum | solution.py:16
  416.5 15.4 %all-reduce.2 = (f32[1024]{0:T(1024)S(1)}, f32[1024]{0:T(1024)S(1)}, f32[1024]{0:T(1024)S(1)}, f32[1024]{0:T(1024)S(1)}, f32[1024]{0:T(1024)S(1)}) all-reduce(f32[1024]{0:T(1024)S(1)} %get-tuple-element.9, f32[1024]{0:T(1024)S(1)} %get-tuple-element.10, ...), channel_id=1, replica_groups=mesh['dp_0'=8,'dp_1'=2,'mp_0'=8,'mp_1'=4] {'mp_1'}, use_global_device_ids=true, to_apply=%region_11.0 | all-reduce | flops 5120 | bytes 40960 | tf_op jit(solution)/shard_map/psum | solution.py:16
  431.9 1.8 subtract_subtract_fusion
  433.7 1.3 copy.10
  435.0 0.7 fusion.11
  (10 shorter events, 0.0 us)
Async XLA Ops:
  0.6 346.9 %copy-start = (bf16[256,3584]{1,0:T(8,128)(2,1)S(1)}, bf16[256,3584]{1,0:T(8,128)(2,1)}, u32[]{:S(2)}) copy-start(bf16[256,3584]{1,0:T(8,128)(2,1)} %param.13) | copy-start | bytes 5505028
  11.7 10.6 %copy-start.2 = (f32[1024]{0:T(1024)S(1)}, f32[1024]{0:T(1024)}, u32[]{:S(2)}) copy-start(f32[1024]{0:T(1024)} %param.14) | copy-start | bytes 12292
  11.7 10.6 %copy-start.3 = (s32[1024]{0:T(1024)S(1)}, s32[1024]{0:T(1024)}, u32[]{:S(2)}) copy-start(s32[1024]{0:T(1024)} %param.15) | copy-start | bytes 12292
  11.7 329.6 %all-to-all-start = ((bf16[16,2,64,3584]{3,2,1,0:T(8,128)(2,1)}), bf16[16,2,64,3584]{3,2,1,0:T(8,128)(2,1)}, u32[]{:S(2)}, u32[]{:S(2)}) async-start(bf16[16,2,64,3584]{3,2,1,0:T(8,128)(2,1)} %stack.25), calls=%async_computation | async-start | bytes 29360128 | tf_op jit(solution)/shard_map/all_to_all | solution.py:48
  347.5 2.1 copy-start.4
  352.0 1.4 copy-start.1
